TPU v7x, 512 devices: a whole 4x8x8 slice. The times are simulated.
512 devices in a mesh: dp: 16 (over y, core), tensor: 32 (over z, x).
Axes of the slice: x: 4, y: 8, z: 8, core: 2. Of those that a mesh axis runs over, the one named last changes fastest.
Arguments:
- tokens: bfloat16 [5632, 4096], P('dp', 'tensor'), may hold values from -6 to 6
- grad_out: bfloat16 [5632, 4096], P('dp', 'tensor'), may hold values from -6 to 6
- routes: float32 [16, 2, 16], P('dp'), may hold values from 0.005 to 0.3
- counts: int32 [16], P('dp'), may hold values from 176 to 352
- up_weight: bfloat16 [16, 4096, 4096], P(None, 'dp', 'tensor'), may hold values from -0.09375 to 0.09375
- down_weight: bfloat16 [16, 4096, 4096], P(None, 'tensor', 'dp'), may hold values from -0.09375 to 0.09375
Outputs:
- input_grad: bfloat16 [5632, 4096], P('dp', 'tensor')
- up_grad: bfloat16 [16, 4096, 4096], P(None, 'dp', 'tensor')
- down_grad: bfloat16 [16, 4096, 4096], P(None, 'tensor', 'dp')
- route_grad: float32 [16, 2, 16], P('dp')
Inputs may be any that keep to these rules, and one draw needn't show every extreme that they name: `counts`: the valid tokens of a data group, at least one whole segment.
All inputs are finite; a program needn't handle non-finite values.
Results may differ from a plain program's by a relative error of at most 0.02.
Values may be sent and summed in bfloat16 or wider, within the bound.
No kernel may reach another device: no remote copies, remote signals or barrier semaphores. Data moves between devices by JAX's collectives and lax.ppermute only.
A program may use at most 64 MiB of HBM per device.

v0:
```python
import jax
import jax.numpy as jnp
from jax import lax
from jax.sharding import PartitionSpec as P

gelu_scale = 0.7978845608
gelu_cubic = 0.044715


def gelu_pair(inputs):
    inner = gelu_scale * (inputs + gelu_cubic * inputs * inputs * inputs)
    tangent = jnp.tanh(inner)
    activated = 0.5 * inputs * (1.0 + tangent)
    derivative = 0.5 * (1.0 + tangent) + 0.5 * inputs * (1.0 - tangent * tangent) * gelu_scale * (
        1.0 + 3.0 * gelu_cubic * inputs * inputs
    )
    return (activated, derivative)


def body(tokens, grad_out, routes, counts, up_weight, down_weight):
    group_rows = tokens.shape[0]
    experts = up_weight.shape[0]
    segments = routes.shape[1]
    seg_rows = group_rows // segments
    high = lax.Precision.HIGHEST
    valid = (jnp.arange(group_rows, dtype=jnp.int32) < counts[0])[:, None]
    masked = jnp.where(valid, grad_out, jnp.zeros_like(grad_out))
    full_tokens, full_grads = (
        lax.all_gather(tokens, "tensor", axis=1, tiled=True),
        lax.all_gather(masked, "tensor", axis=1, tiled=True),
    )
    all_routes = lax.all_gather(routes, "dp", axis=0, tiled=True)
    flat_routes = all_routes.reshape(-1, experts)
    local_up = jnp.dot(
        flat_routes, up_weight.reshape(experts, -1).astype(jnp.float32), precision=high
    )
    local_up = local_up.reshape((-1,) + up_weight.shape[1:]).astype(jnp.bfloat16)
    down_turned = jnp.swapaxes(down_weight, 1, 2)
    local_down = jnp.dot(
        flat_routes, down_turned.reshape(experts, -1).astype(jnp.float32), precision=high
    )
    local_down = local_down.reshape((-1,) + down_turned.shape[1:]).astype(jnp.bfloat16)
    merged_up, merged_down = (
        lax.all_to_all(local_up, "dp", split_axis=0, concat_axis=1, tiled=True),
        lax.all_to_all(local_down, "dp", split_axis=0, concat_axis=1, tiled=True),
    )
    down_terms = []
    slopes = []
    for segment in range(segments):
        seg_tokens = full_tokens[segment * seg_rows : (segment + 1) * seg_rows]
        seg_grads = full_grads[segment * seg_rows : (segment + 1) * seg_rows]
        pre = jnp.dot(seg_tokens, merged_up[segment], preferred_element_type=jnp.float32)
        activated, derivative = gelu_pair(pre)
        activated = activated.astype(jnp.bfloat16)
        slopes.append(derivative)
        down_terms.append(
            jnp.einsum(
                "rd,rh->dh", seg_grads, activated, preferred_element_type=jnp.float32
            ).astype(jnp.bfloat16)
        )
    down_stack = jnp.stack(down_terms, axis=0)
    up_terms = []
    hidden_grads = []
    for segment in range(segments):
        seg_tokens = full_tokens[segment * seg_rows : (segment + 1) * seg_rows]
        seg_grads = full_grads[segment * seg_rows : (segment + 1) * seg_rows]
        back = jnp.einsum(
            "rd,dh->rh", seg_grads, merged_down[segment], preferred_element_type=jnp.float32
        )
        hidden_grad = (back * slopes[segment]).astype(jnp.bfloat16)
        hidden_grads.append(hidden_grad)
        up_terms.append(
            jnp.einsum(
                "rd,rh->dh", seg_tokens, hidden_grad, preferred_element_type=jnp.float32
            ).astype(jnp.bfloat16)
        )
    up_stack = jnp.stack(up_terms, axis=0)
    recv_up, recv_down = (
        lax.all_to_all(up_stack, "dp", split_axis=1, concat_axis=0, tiled=True),
        lax.all_to_all(down_stack, "dp", split_axis=1, concat_axis=0, tiled=True),
    )
    partials = [
        jnp.einsum(
            "rh,dh->rd",
            hidden_grads[segment],
            merged_up[segment],
            preferred_element_type=jnp.float32,
        )
        for segment in range(segments)
    ]
    rounded = lax.optimization_barrier(jnp.concatenate(partials, axis=0).astype(jnp.bfloat16))
    summed = lax.psum_scatter(
        rounded.astype(jnp.float32).astype(jnp.bfloat16), "tensor", scatter_dimension=1, tiled=True
    )
    up_grad = jnp.einsum(
        "ke,kdh->edh", flat_routes, recv_up.astype(jnp.float32), precision=high
    ).astype(jnp.bfloat16)
    down_grad = jnp.einsum(
        "ke,kdh->ehd", flat_routes, recv_down.astype(jnp.float32), precision=high
    ).astype(jnp.bfloat16)
    inner_sums = jnp.einsum("kdh,edh->ke", recv_up, up_weight, preferred_element_type=jnp.float32)
    inner_sums = inner_sums + jnp.einsum(
        "kdh,ehd->ke", recv_down, down_weight, preferred_element_type=jnp.float32
    )
    table = inner_sums.reshape(all_routes.shape)
    totals = lax.psum(table, ("dp", "tensor"))
    route_grad = lax.dynamic_slice_in_dim(totals, lax.axis_index("dp"), 1, 0)
    return (summed, up_grad, down_grad, route_grad)


def solution(mesh):
    return jax.shard_map(
        body,
        mesh=mesh,
        in_specs=(
            P("dp", "tensor"),
            P("dp", "tensor"),
            P("dp", None, None),
            P("dp"),
            P(None, "dp", "tensor"),
            P(None, "tensor", "dp"),
        ),
        out_specs=(
            P("dp", "tensor"),
            P(None, "dp", "tensor"),
            P(None, "tensor", "dp"),
            P("dp", None, None),
        ),
        check_vma=False,
    )
```

profile of v0, /device:TPU:8, one launch (start us, length us, event | category | flops | bytes accessed | tf_op | source)
XLA Modules:
  0.0 445.9 jit_solution(14864564712320135347)
XLA Ops:
  7.2 0.0 all-gather.5.cloned.1.call-start
  7.2 0.7 all-gather.5.cloned.1.call-update
  7.9 20.2 %all_gather.10 = f32[16,2,16]{2,1,0:T(2,128)S(1)} all-gather(f32[1,2,16]{2,1,0:T(2,128)} %param.8), channel_id=1, replica_groups=mesh['dp'=16,'tensor'=32] {'dp'}, dimensions={0}, use_global_device_ids=true | all-gather | bytes 2176 | tf_op jit(solution)/shard_map/all_gather | solution.py:32
  28.1 3.1 convolution_convert_fusion.6
  31.2 2.2 copy.65
  33.4 0.0 copy-start.7
  33.4 3.8 all-to-all-start.1
  37.1 0.0 all-gather.3.cloned.1.call-start
  37.8 0.0 copy-done.7
  37.8 0.8 broadcast_select_fusion
  38.6 0.0 all-gather.3.cloned.1.call-update
  38.6 1.6 copy.59
  40.2 1.9 convolution_convert_fusion.7
  42.1 2.2 copy.62
  44.3 40.2 %all-to-all-done.1 = bf16[32,256,128]{2,1,0:T(8,128)(2,1)S(1)} async-done(((bf16[32,256,128]{2,1,0:T(8,128)(2,1)}), bf16[32,256,128]{2,1,0:T(8,128)(2,1)S(1)}, u32[]{:S(2)}, u32[]{:S(2)}) %all-to-all-start.1) | async-done | bytes 2097184 | tf_op jit(solution)/shard_map/all_to_all | solution.py:44
  84.5 6.6 %all-to-all-start = ((bf16[32,256,128]{2,1,0:T(8,128)(2,1)}), bf16[32,256,128]{2,1,0:T(8,128)(2,1)}, u32[]{:S(2)}, u32[]{:S(2)}) async-start(bf16[32,256,128]{2,1,0:T(8,128)(2,1)} %copy.62), calls=%async_computation | async-start | bytes 4194304 | tf_op jit(solution)/shard_map/all_to_all | solution.py:45
  91.1 1.2 fusion.98
  92.3 46.3 %all-to-all-done = bf16[32,256,128]{2,1,0:T(8,128)(2,1)} async-done(((bf16[32,256,128]{2,1,0:T(8,128)(2,1)}), bf16[32,256,128]{2,1,0:T(8,128)(2,1)}, u32[]{:S(2)}, u32[]{:S(2)}) %all-to-all-start) | async-done | bytes 2097184 | tf_op jit(solution)/shard_map/all_to_all | solution.py:45
  138.6 2.8 fusion.99
  141.4 0.0 copy-done.1
  141.4 1.9 fusion.39
  143.3 43.1 %all-gather.3.cloned.1.call-done = bf16[352,4096]{1,0:T(8,128)(2,1)} async-done(((bf16[352,128]{1,0:T(8,128)(2,1)}), bf16[352,4096]{1,0:T(8,128)(2,1)}) %all-gather.3.cloned.1.call-update) | async-done | bytes 2883600 | tf_op jit(solution)/shard_map/all_gather | solution.py:30
  186.4 2.3 fusion.51
  188.7 0.2 copy-done.3
  189.0 0.5 fusion
  189.4 0.5 fusion.45
  190.0 0.8 copy-done.2
  190.8 0.5 fusion.48
  191.3 0.5 fusion.1
  191.8 0.2 pad_maximum_fusion.1
  192.0 3.8 copy.66
  195.8 7.3 %all-to-all-start.2 = ((bf16[2,4096,128]{2,0,1:T(2,128)(2,1)}), bf16[2,4096,128]{2,0,1:T(2,128)(2,1)S(1)}, u32[]{:S(2)}, u32[]{:S(2)}) async-start(bf16[2,4096,128]{2,0,1:T(2,128)(2,1)} %copy.66), calls=%async_computation.2 | async-start | bytes 4194304 | tf_op jit(solution)/shard_map/all_to_all | solution.py:79
  203.1 0.2 reduce-scatter.4.cloned.1.call-start
  203.3 1.8 convolution_convert_fusion.1
  205.0 0.5 convolution_convert_fusion
  205.6 1.8 pad_maximum_fusion
  207.4 4.6 %copy.95 = bf16[352,4096]{0,1:T(8,128)(2,1)} copy(bf16[352,4096]{1,0:T(8,128)(2,1)} %pad_maximum_fusion) | data formatting | bytes 5767168
  212.0 0.0 reduce-scatter.4.cloned.1.call-update
  212.0 2.1 fusion.2
  214.2 2.1 fusion.3
  216.3 0.2 pad_maximum_fusion.2
  216.5 18.1 %copy.70 = bf16[2,4096,128]{2,0,1:T(2,128)(2,1)} copy(bf16[2,4096,128]{2,1,0:T(8,128)(2,1)S(1)} %pad_maximum_fusion.2) | data formatting | bytes 4194304 | tf_op jit(solution)/shard_map/stack | solution.py:61
  234.6 15.8 %all-to-all-done.2 = bf16[2,4096,128]{2,0,1:T(2,128)(2,1)S(1)} async-done(((bf16[2,4096,128]{2,0,1:T(2,128)(2,1)}), bf16[2,4096,128]{2,0,1:T(2,128)(2,1)S(1)}, u32[]{:S(2)}, u32[]{:S(2)}) %all-to-all-start.2) | async-done | bytes 2097184 | tf_op jit(solution)/shard_map/all_to_all | solution.py:79
  250.4 6.5 %all-to-all-start.3 = ((bf16[2,4096,128]{2,0,1:T(2,128)(2,1)}), bf16[2,4096,128]{2,0,1:T(2,128)(2,1)}, u32[]{:S(2)}, u32[]{:S(2)}) async-start(bf16[2,4096,128]{2,0,1:T(2,128)(2,1)} %copy.70), calls=%async_computation.3 | async-start | bytes 4194304 | tf_op jit(solution)/shard_map/all_to_all | solution.py:80
  257.0 0.0 copy-done
  257.0 1.8 copy.79
  258.8 1.9 copy.93
  260.7 43.8 %all-to-all-done.3 = bf16[2,4096,128]{2,0,1:T(2,128)(2,1)} async-done(((bf16[2,4096,128]{2,0,1:T(2,128)(2,1)}), bf16[2,4096,128]{2,0,1:T(2,128)(2,1)}, u32[]{:S(2)}, u32[]{:S(2)}) %all-to-all-start.3) | async-done | bytes 2097184 | tf_op jit(solution)/shard_map/all_to_all | solution.py:80
  304.5 2.3 copy.94
  306.7 0.0 copy-start.6
  306.8 0.0 copy-done.4
  306.8 0.2 copy-done.5
  307.0 2.0 fusion.54
  309.0 0.0 copy-done.6
  309.0 1.3 fusion.60
  310.3 0.1 copy.80
  310.4 1.9 fusion.18
  312.3 1.2 copy.81
  313.6 3.5 fusion.21
  317.1 1.6 copy.82
  318.6 98.9 %psum.7 = f32[16,2,16]{2,1,0:T(2,128)S(1)} all-reduce(f32[16,2,16]{2,1,0:T(2,128)S(1)} %bitcast.141), channel_id=1, replica_groups=mesh['dp'=16,'tensor'=32] {'dp','tensor'}, use_global_device_ids=true, to_apply=%region_1.2 | all-reduce | flops 512 | bytes 4096 | tf_op jit(solution)/shard_map/psum | solution.py:106
  417.5 0.6 constant_dynamic-slice_fusion
  418.1 19.6 %reduce-scatter.4.cloned.1.call-done = bf16[128,352]{1,0:T(8,128)(2,1)} async-done(((bf16[4096,352]{1,0:T(8,128)(2,1)}), bf16[128,352]{1,0:T(8,128)(2,1)}) %reduce-scatter.4.cloned.1.call-update) | async-done | bytes 90128
  437.8 1.6 copy.96
  (8 shorter events, 0.0 us)
Async XLA Ops:
  7.2 134.2 %all-gather.5.cloned.1.call-start = ((), (), s32[]{:S(2)}) async-start(), calls=%async_computation.6 | async-start | bytes 2973696 | tf_op jit(solution)/shard_map/all_gather | solution.py:29
  33.4 4.5 %copy-start.7 = (bf16[352,128]{1,0:T(8,128)(2,1)S(1)}, bf16[352,128]{1,0:T(8,128)(2,1)}, u32[]{:S(2)}) copy-start(bf16[352,128]{1,0:T(8,128)(2,1)} %param.7) | copy-start | bytes 270340
  33.4 51.2 %all-to-all-start.1 = ((bf16[32,256,128]{2,1,0:T(8,128)(2,1)}), bf16[32,256,128]{2,1,0:T(8,128)(2,1)S(1)}, u32[]{:S(2)}, u32[]{:S(2)}) async-start(bf16[32,256,128]{2,1,0:T(8,128)(2,1)} %copy.65), calls=%async_computation.1 | async-start | bytes 4194304 | tf_op jit(solution)/shard_map/all_to_all | solution.py:44
  37.1 149.3 %all-gather.3.cloned.1.call-start = ((), (), s32[]{:S(2)}) async-start(), calls=%async_computation.5 | async-start | bytes 2973696 | tf_op jit(solution)/shard_map/all_gather | solution.py:30
  84.5 54.1 %all-to-all-start = ((bf16[32,256,128]{2,1,0:T(8,128)(2,1)}), bf16[32,256,128]{2,1,0:T(8,128)(2,1)}, u32[]{:S(2)}, u32[]{:S(2)}) async-start(bf16[32,256,128]{2,1,0:T(8,128)(2,1)} %copy.62), calls=%async_computation | async-start | bytes 4194304 | tf_op jit(solution)/shard_map/all_to_all | solution.py:45
  138.6 2.8 copy-start.1
  186.4 2.6 copy-start.3
  189.0 1.8 copy-start.2
  195.8 54.7 %all-to-all-start.2 = ((bf16[2,4096,128]{2,0,1:T(2,128)(2,1)}), bf16[2,4096,128]{2,0,1:T(2,128)(2,1)S(1)}, u32[]{:S(2)}, u32[]{:S(2)}) async-start(bf16[2,4096,128]{2,0,1:T(2,128)(2,1)} %copy.66), calls=%async_computation.2 | async-start | bytes 4194304 | tf_op jit(solution)/shard_map/all_to_all | solution.py:79
  203.1 234.7 %reduce-scatter.4.cloned.1.call-start = ((), (), s32[]{:S(2)}) async-start(), calls=%async_computation.7 | async-start | bytes 3244032
  234.6 22.4 %copy-start = (bf16[16,128,256]{2,1,0:T(8,128)(2,1)S(1)}, bf16[16,128,256]{2,1,0:T(8,128)(2,1)}, u32[]{:S(2)}) copy-start(bf16[16,128,256]{2,1,0:T(8,128)(2,1)} %param.11) | copy-start | bytes 3145732
  250.4 54.0 %all-to-all-start.3 = ((bf16[2,4096,128]{2,0,1:T(2,128)(2,1)}), bf16[2,4096,128]{2,0,1:T(2,128)(2,1)}, u32[]{:S(2)}, u32[]{:S(2)}) async-start(bf16[2,4096,128]{2,0,1:T(2,128)(2,1)} %copy.70), calls=%async_computation.3 | async-start | bytes 4194304 | tf_op jit(solution)/shard_map/all_to_all | solution.py:80
  304.5 2.3 copy-start.4
  304.5 2.5 copy-start.5
  306.7 2.3 copy-start.6
Sparse Core Ops, SparseCore 0:
  11.0 88.2 all-gather.4
  103.0 83.3 all-gather.2
  212.1 225.5 reduce-scatter.3
where the time goes:
time: 447 us; the launch traced here: 446 us
  waiting for transfers between devices  210 us (47%)
  blocking collectives  119 us (27%)
  local copies, waits for them, and re-layouts  48.7 us (11%)
  matrix products  26.5 us (6%)
  starting transfers between devices  24.5 us (5%)
  between operations  14.6 us (3%)
    psum x1, blocking collectives, body(): totals = lax.psum(table, ('dp', 'tensor'))  98.9 us
    all_to_all x1, waiting for transfers between devices, body(): lax.all_to_all(local_down, 'dp', split_axis=0, concat_axis=1, tiled=True)  46.3 us
    all_to_all x1, waiting for transfers between devices, body(): lax.all_to_all(down_stack, 'dp', split_axis=1, concat_axis=0, tiled=True)  43.8 us
    all_gather x1, waiting for transfers between devices, body(): lax.all_gather(masked, 'tensor', axis=1, tiled=True)  43.1 us
    all_to_all x1, waiting for transfers between devices, body(): lax.all_to_all(local_up, 'dp', split_axis=0, concat_axis=1, tiled=True)  40.2 us
    unnamed x4, waiting for transfers between devices  20.4 us
    all_gather x1, blocking collectives, body(): all_routes = lax.all_gather(routes, 'dp', axis=0, tiled=True)  20.2 us
    another operation x1, local copies, waits for them, and re-layouts, body(): down_stack = jnp.stack(down_terms, axis=0)  18.1 us
  transfers between devices with their start and end apart: 7, of which 6 were waited for; matrix products, arithmetic and copies ran while one was open for 15% of the time, Pallas kernels for 0%

commit v1 on v0

--- a/solution.py
+++ b/solution.py
@@ -103,7 +103,7 @@
         "kdh,ehd->ke", recv_down, down_weight, preferred_element_type=jnp.float32
     )
     table = inner_sums.reshape(all_routes.shape)
-    totals = lax.psum(table, ("dp", "tensor"))
+    totals = lax.all_gather(table, ("dp", "tensor")).sum(axis=0)
     route_grad = lax.dynamic_slice_in_dim(totals, lax.axis_index("dp"), 1, 0)
     return (summed, up_grad, down_grad, route_grad)
 

time: 447 us -> 581 us (1.30)
  the two profiles are of different devices: /device:TPU:8 before, /device:TPU:1 now
where the time goes in v1:
time: 581 us; the launch traced here: 580 us
  waiting for transfers between devices  438 us (75%)
  local copies, waits for them, and re-layouts  48.1 us (8%)
  matrix products  27 us (5%)
  starting transfers between devices  24.2 us (4%)
  blocking collectives  20.9 us (4%)
  between operations  14.7 us (3%)
  other arithmetic  6.91 us (1%)
    all_gather x1, waiting for transfers between devices, body(): totals = lax.all_gather(table, ('dp', 'tensor')).sum(axis=0)  135 us
    unnamed x5, waiting for transfers between devices  112 us
    all_to_all x1, waiting for transfers between devices, body(): lax.all_to_all(local_up, 'dp', split_axis=0, concat_axis=1, tiled=True)  47.6 us
    all_to_all x1, waiting for transfers between devices, body(): lax.all_to_all(down_stack, 'dp', split_axis=1, concat_axis=0, tiled=True)  45.2 us
    all_to_all x1, waiting for transfers between devices, body(): lax.all_to_all(local_down, 'dp', split_axis=0, concat_axis=1, tiled=True)  43.4 us
    all_gather x1, waiting for transfers between devices, body(): lax.all_gather(masked, 'tensor', axis=1, tiled=True)  37.6 us
    all_gather x1, blocking collectives, body(): all_routes = lax.all_gather(routes, 'dp', axis=0, tiled=True)  20.9 us
    another operation x1, local copies, waits for them, and re-layouts, body(): down_stack = jnp.stack(down_terms, axis=0)  18.1 us
  transfers between devices with their start and end apart: 8, of which 7 were waited for; matrix products, arithmetic and copies ran while one was open for 12% of the time, Pallas kernels for 0%

profile of v1, /device:TPU:1, one launch (start us, length us, event | category | flops | bytes accessed | tf_op | source)
XLA Modules:
  0.0 579.9 jit_solution(2774708037847643910)
XLA Ops:
  7.2 0.0 all-gather.6.cloned.1.call-start
  7.2 0.7 all-gather.6.cloned.1.call-update
  7.9 1.6 copy.84
  9.5 20.9 %all_gather.13 = f32[16,2,16]{2,1,0:T(2,128)S(1)} all-gather(f32[1,2,16]{2,1,0:T(2,128)S(1)} %copy-done.10), channel_id=1, replica_groups=mesh['dp'=16,'tensor'=32] {'dp'}, dimensions={0}, use_global_device_ids=true | all-gather | bytes 2176 | tf_op jit(solution)/shard_map/all_gather | solution.py:32
  30.4 1.9 convolution_convert_fusion.7
  32.3 2.2 copy.87
  34.5 3.8 all-to-all-start
  38.3 0.0 all-gather.4.cloned.1.call-start
  39.0 0.8 broadcast_select_fusion
  39.8 0.0 all-gather.4.cloned.1.call-update
  39.8 1.9 convolution_convert_fusion.6
  41.7 2.2 copy.90
  43.9 43.4 %all-to-all-done = bf16[32,256,128]{2,1,0:T(8,128)(2,1)S(1)} async-done(((bf16[32,256,128]{2,1,0:T(8,128)(2,1)}), bf16[32,256,128]{2,1,0:T(8,128)(2,1)S(1)}, u32[]{:S(2)}, u32[]{:S(2)}) %all-to-all-start) | async-done | bytes 2097184 | tf_op jit(solution)/shard_map/all_to_all | solution.py:45
  87.3 5.0 all-to-all-start.1
  92.3 1.5 fusion.99
  93.7 47.6 %all-to-all-done.1 = bf16[32,256,128]{2,1,0:T(8,128)(2,1)} async-done(((bf16[32,256,128]{2,1,0:T(8,128)(2,1)}), bf16[32,256,128]{2,1,0:T(8,128)(2,1)}, u32[]{:S(2)}, u32[]{:S(2)}) %all-to-all-start.1) | async-done | bytes 2097184 | tf_op jit(solution)/shard_map/all_to_all | solution.py:44
  141.3 1.7 fusion.98
  143.0 0.0 all-gather.6.cloned.1.call-done
  143.1 2.2 fusion.45
  145.3 0.0 copy-start.8
  145.3 2.0 fusion.39
  147.3 37.6 %all-gather.4.cloned.1.call-done = bf16[352,4096]{1,0:T(8,128)(2,1)} async-done(((bf16[352,128]{1,0:T(8,128)(2,1)}), bf16[352,4096]{1,0:T(8,128)(2,1)}) %all-gather.4.cloned.1.call-update) | async-done | bytes 2883600 | tf_op jit(solution)/shard_map/all_gather | solution.py:30
  184.9 2.3 fusion.48
  187.2 0.2 copy-done.3
  187.5 0.5 fusion.1
  187.9 0.4 copy-done.2
  188.3 0.5 fusion.51
  188.9 0.5 fusion
  189.3 0.2 pad_maximum_fusion.1
  189.5 3.8 copy.91
  193.3 9.9 %all-to-all-start.2 = ((bf16[2,4096,128]{2,0,1:T(2,128)(2,1)}), bf16[2,4096,128]{2,0,1:T(2,128)(2,1)S(1)}, u32[]{:S(2)}, u32[]{:S(2)}) async-start(bf16[2,4096,128]{2,0,1:T(2,128)(2,1)} %copy.91), calls=%async_computation.2 | async-start | bytes 4194304 | tf_op jit(solution)/shard_map/all_to_all | solution.py:79
  203.2 0.2 reduce-scatter.4.cloned.1.call-start
  203.4 1.8 convolution_convert_fusion
  205.2 0.5 convolution_convert_fusion.1
  205.7 1.8 pad_maximum_fusion
  207.5 4.7 copy.122
  212.2 0.0 reduce-scatter.4.cloned.1.call-update
  212.2 2.1 fusion.3
  214.3 2.1 fusion.2
  216.5 0.2 pad_maximum_fusion.2
  216.7 18.1 %copy.95 = bf16[2,4096,128]{2,0,1:T(2,128)(2,1)} copy(bf16[2,4096,128]{2,1,0:T(8,128)(2,1)S(1)} %pad_maximum_fusion.2) | data formatting | bytes 4194304 | tf_op jit(solution)/shard_map/stack | solution.py:61
  234.8 17.3 %all-to-all-done.2 = bf16[2,4096,128]{2,0,1:T(2,128)(2,1)S(1)} async-done(((bf16[2,4096,128]{2,0,1:T(2,128)(2,1)}), bf16[2,4096,128]{2,0,1:T(2,128)(2,1)S(1)}, u32[]{:S(2)}, u32[]{:S(2)}) %all-to-all-start.2) | async-done | bytes 2097184 | tf_op jit(solution)/shard_map/all_to_all | solution.py:79
  252.1 5.0 all-to-all-start.3
  257.1 0.3 all-gather.8.cloned.1.call-start
  257.4 1.8 copy.104
  259.2 1.8 copy.120
  261.0 45.2 %all-to-all-done.3 = bf16[2,4096,128]{2,0,1:T(2,128)(2,1)} async-done(((bf16[2,4096,128]{2,0,1:T(2,128)(2,1)}), bf16[2,4096,128]{2,0,1:T(2,128)(2,1)}, u32[]{:S(2)}, u32[]{:S(2)}) %all-to-all-start.3) | async-done | bytes 2097184 | tf_op jit(solution)/shard_map/all_to_all | solution.py:80
  306.2 2.2 copy.121
  308.4 0.0 copy-start.7
  308.4 0.2 copy-done.6
  308.7 2.0 fusion.54
  310.7 1.3 fusion.60
  312.0 0.1 copy.105
  312.1 0.6 copy.106
  312.7 0.0 all-gather.8.cloned.1.call-update
  312.8 1.9 fusion.18
  314.7 1.2 copy.107
  315.9 3.5 fusion.21
  319.4 1.6 copy.108
  321.0 111.7 %reduce-scatter.4.cloned.1.call-done = bf16[128,352]{1,0:T(8,128)(2,1)} async-done(((bf16[4096,352]{1,0:T(8,128)(2,1)}), bf16[128,352]{1,0:T(8,128)(2,1)}) %reduce-scatter.4.cloned.1.call-update) | async-done | bytes 90128
  432.6 1.6 copy.123
  434.3 134.6 %all-gather.8.cloned.1.call-done = f32[512,16,2,16]{3,1,2,0:T(8,128)} async-done(((f32[1,16,2,16]{3,1,2,0:T(8,128)}), f32[512,16,2,16]{3,1,2,0:T(8,128)}) %all-gather.8.cloned.1.call-update) | async-done | bytes 1048592 | tf_op jit(solution)/shard_map/all_gather | solution.py:106
  568.8 4.0 reduce_sum.9
  572.8 0.6 constant_dynamic-slice_fusion
  (18 shorter events, 0.0 us)
Async XLA Ops:
  7.2 2.4 copy-start.10
  7.2 135.9 %all-gather.6.cloned.1.call-start = ((), (), s32[]{:S(2)}) async-start(), calls=%async_computation.6 | async-start | bytes 2973696 | tf_op jit(solution)/shard_map/all_gather | solution.py:29
  34.5 4.5 copy-start.9
  34.5 5.3 copy-start.5
  34.5 52.8 %all-to-all-start = ((bf16[32,256,128]{2,1,0:T(8,128)(2,1)}), bf16[32,256,128]{2,1,0:T(8,128)(2,1)S(1)}, u32[]{:S(2)}, u32[]{:S(2)}) async-start(bf16[32,256,128]{2,1,0:T(8,128)(2,1)} %copy.87), calls=%async_computation | async-start | bytes 4194304 | tf_op jit(solution)/shard_map/all_to_all | solution.py:45
  38.3 146.6 %all-gather.4.cloned.1.call-start = ((), (), s32[]{:S(2)}) async-start(), calls=%async_computation.5 | async-start | bytes 2973696 | tf_op jit(solution)/shard_map/all_gather | solution.py:30
  87.3 54.1 %all-to-all-start.1 = ((bf16[32,256,128]{2,1,0:T(8,128)(2,1)}), bf16[32,256,128]{2,1,0:T(8,128)(2,1)}, u32[]{:S(2)}, u32[]{:S(2)}) async-start(bf16[32,256,128]{2,1,0:T(8,128)(2,1)} %copy.90), calls=%async_computation.1 | async-start | bytes 4194304 | tf_op jit(solution)/shard_map/all_to_all | solution.py:44
  143.0 4.3 copy-start.1
  145.3 42.6 %copy-start.8 = (bf16[1,16,256,128]{3,2,0,1:T(8,128)(2,1)S(1)}, bf16[1,16,256,128]{3,2,0,1:T(8,128)(2,1)}, u32[]{:S(2)}) copy-start(bf16[1,16,256,128]{3,2,0,1:T(8,128)(2,1)} %get-tuple-element.26) | copy-start | bytes 3145732
  184.9 2.6 copy-start.3
  184.9 3.4 copy-start.2
  193.3 58.8 %all-to-all-start.2 = ((bf16[2,4096,128]{2,0,1:T(2,128)(2,1)}), bf16[2,4096,128]{2,0,1:T(2,128)(2,1)S(1)}, u32[]{:S(2)}, u32[]{:S(2)}) async-start(bf16[2,4096,128]{2,0,1:T(2,128)(2,1)} %copy.91), calls=%async_computation.2 | async-start | bytes 4194304 | tf_op jit(solution)/shard_map/all_to_all | solution.py:79
  203.2 229.5 %reduce-scatter.4.cloned.1.call-start = ((), (), s32[]{:S(2)}) async-start(), calls=%async_computation.8 | async-start | bytes 3244032
  234.8 22.6 %copy-start = (bf16[16,128,256]{2,1,0:T(8,128)(2,1)S(1)}, bf16[16,128,256]{2,1,0:T(8,128)(2,1)}, u32[]{:S(2)}) copy-start(bf16[16,128,256]{2,1,0:T(8,128)(2,1)} %param.11) | copy-start | bytes 3145732
  252.1 54.0 %all-to-all-start.3 = ((bf16[2,4096,128]{2,0,1:T(2,128)(2,1)}), bf16[2,4096,128]{2,0,1:T(2,128)(2,1)}, u32[]{:S(2)}, u32[]{:S(2)}) async-start(bf16[2,4096,128]{2,0,1:T(2,128)(2,1)} %copy.95), calls=%async_computation.3 | async-start | bytes 4194304 | tf_op jit(solution)/shard_map/all_to_all | solution.py:80
  257.1 311.7 %all-gather.8.cloned.1.call-start = ((), (), s32[]{:S(2)}) async-start(), calls=%async_computation.7 | async-start | bytes 8404992 | tf_op jit(solution)/shard_map/all_gather | solution.py:106
  306.2 2.3 copy-start.4
  306.2 2.5 copy-start.6
  308.4 2.3 copy-start.7
Sparse Core Ops, SparseCore 0:
  11.1 86.7 all-gather.5
  101.5 83.3 all-gather.3
  212.3 220.2 reduce-scatter.3
  437.7 131.0 all-gather.7
